TPU v7x, 32 devices: a whole 2x2x4 slice. The times are simulated.
32 devices in a mesh: dp: 4 (over z), adapter: 2 (over x), fsdp: 4 (over y, core).
Axes of the slice: x: 2, y: 2, z: 4, core: 2. Of those that a mesh axis runs over, the one named last changes fastest.
Arguments:
- adapter_index: int32 [768], P(('dp', 'adapter', 'fsdp')), may hold values from 0 to 1, as said below
- output_gradient: bfloat16 [768, 4096], P(('dp', 'adapter', 'fsdp')), may hold values from -6 to 6
- hidden: bfloat16 [768, 14336], P(('dp', 'adapter', 'fsdp')), may hold values from -6 to 6
- frozen_down_weight: bfloat16 [14336, 4096], P('adapter', 'fsdp'), may hold values from -0.046875 to 0.046875
- adapter_input_maps: bfloat16 [2, 16, 14336], P('adapter'), may hold values from -0.046875 to 0.046875
- adapter_output_maps: bfloat16 [2, 16, 4096], P('adapter'), may hold values from -1.5 to 1.5
Outputs:
- hidden_gradient: bfloat16 [768, 14336], P(('dp', 'adapter', 'fsdp'))
- adapter_input_gradient: float32 [2, 16, 14336], P('adapter')
- adapter_output_gradient: float32 [2, 16, 4096], P('adapter')
Inputs may be any that keep to these rules, and one draw needn't show every extreme that they name: `adapter_index`: adapter i sits at index i // 1 of adapter. Of the 24 tokens of one device (aligned blocks of 24 rows), at most 12 name adapters at the same index; in every draw one index is named by exactly 12 tokens of every device.
All inputs are finite; a program needn't handle non-finite values.
Results may differ from a plain program's by a relative error of at most 0.015.
Values may be sent and summed in bfloat16 or wider, within the bound.
A program may use at most 64 MiB of HBM per device.

v0:
```python
import jax
import jax.numpy as jnp
from jax import lax
from jax.sharding import PartitionSpec as P

adapter_scale = 2.0


def on_device(
    adapter_index,
    output_gradient,
    hidden,
    frozen_down_weight,
    adapter_input_maps,
    adapter_output_maps,
):
    tok_rows = output_gradient.shape[0]
    token_tenants = lax.axis_size("adapter")
    fibres = lax.axis_size("fsdp")
    groups = lax.axis_size("dp")
    tenant_token_count = adapter_input_maps.shape[0]
    adapter_rank_size = adapter_input_maps.shape[1]
    hidden_units_width = hidden.shape[1]
    model_dimension_width = output_gradient.shape[1]
    capacity = max(2, min(tok_rows // 2, 2 * tok_rows // token_tenants))
    every_token = tok_rows * token_tenants * fibres * groups
    scaling_factor = adapter_scale * (tenant_token_count * token_tenants) / every_token
    slab_width = frozen_down_weight.shape[1]
    own_columns = lax.all_to_all(output_gradient, "fsdp", split_axis=1, concat_axis=0, tiled=True)
    spread = lax.all_gather(own_columns, "adapter", axis=0, tiled=True)
    blocks = spread.reshape(token_tenants, fibres, tok_rows, slab_width)
    per_fibre = token_tenants * tok_rows
    taken = blocks
    taken = jnp.transpose(taken, (1, 0, 2, 3)).reshape(
        per_fibre * lax.axis_size("fsdp"), slab_width
    )
    partial_base = lax.psum_scatter(
        lax.dot_general(
            taken, frozen_down_weight, (((1,), (1,)), ((), ())), preferred_element_type=jnp.float32
        ).astype(jnp.bfloat16),
        "fsdp",
        scatter_dimension=0,
        tiled=True,
    )
    frozen_term = lax.all_to_all(partial_base, "adapter", split_axis=0, concat_axis=1, tiled=True)
    owner_of = adapter_index // tenant_token_count
    local_of = adapter_index - owner_of * tenant_token_count
    same_owner = owner_of[:, None] == owner_of[None, :]
    earlier = jnp.arange(tok_rows)[None, :] < jnp.arange(tok_rows)[:, None]
    position = jnp.sum((same_owner & earlier).astype(jnp.int32), axis=1)
    slot_of = owner_of * capacity + position
    slot_count = token_tenants * capacity
    placing = (jnp.arange(slot_count, dtype=jnp.int32)[:, None] == slot_of[None, :]).astype(
        jnp.bfloat16
    )
    send_out = jnp.dot(placing, output_gradient, preferred_element_type=jnp.float32).astype(
        jnp.bfloat16
    )
    send_hidden = jnp.dot(placing, hidden, preferred_element_type=jnp.float32).astype(jnp.bfloat16)
    send_tag = jnp.dot(
        placing, (local_of + 1).astype(jnp.bfloat16), preferred_element_type=jnp.float32
    ).astype(jnp.bfloat16)
    recv_out, recv_hidden, recv_tag = (
        lax.all_to_all(send_out, "adapter", split_axis=0, concat_axis=0, tiled=True),
        lax.all_to_all(send_hidden, "adapter", split_axis=0, concat_axis=0, tiled=True),
        lax.all_to_all(send_tag, "adapter", split_axis=0, concat_axis=0, tiled=True),
    )
    flattened_input_map = adapter_input_maps.reshape(
        tenant_token_count * adapter_rank_size, hidden_units_width
    )
    flattened_output_map = adapter_output_maps.reshape(
        tenant_token_count * adapter_rank_size, model_dimension_width
    )
    chosen = (
        recv_tag.astype(jnp.float32)[:, None]
        == (jnp.arange(tenant_token_count) + 1).astype(jnp.float32)[None, :]
    )
    row_mask = jnp.repeat(chosen, adapter_rank_size, axis=1).astype(jnp.float32)
    multiplier = (
        lax.dot_general(
            recv_out,
            flattened_output_map,
            (((1,), (1,)), ((), ())),
            preferred_element_type=jnp.float32,
        )
        * row_mask
    ).astype(jnp.bfloat16)
    low_rank = (
        lax.dot_general(
            recv_hidden,
            flattened_input_map,
            (((1,), (1,)), ((), ())),
            preferred_element_type=jnp.float32,
        )
        * row_mask
    ).astype(jnp.bfloat16)
    adapter_token_rows = (
        adapter_scale * jnp.dot(multiplier, flattened_input_map, preferred_element_type=jnp.float32)
    ).astype(jnp.bfloat16)
    grad_a_part = lax.dot_general(
        multiplier, recv_hidden, (((0,), (0,)), ((), ())), preferred_element_type=jnp.float32
    )
    grad_b_part = lax.dot_general(
        low_rank, recv_out, (((0,), (0,)), ((), ())), preferred_element_type=jnp.float32
    )
    backward_result = lax.all_to_all(
        adapter_token_rows, "adapter", split_axis=0, concat_axis=0, tiled=True
    )
    adapter_selection = lax.dot_general(
        placing, backward_result, (((0,), (0,)), ((), ())), preferred_element_type=jnp.float32
    )
    hidden_gradient = (frozen_term.astype(jnp.float32) + adapter_selection).astype(jnp.bfloat16)
    input_map_total, output_map_total = (
        lax.psum(grad_a_part.astype(jnp.bfloat16), ("dp", "fsdp")).astype(jnp.float32),
        lax.psum(grad_b_part.astype(jnp.bfloat16), ("dp", "fsdp")).astype(jnp.float32),
    )
    adapter_input_gradient = (scaling_factor * input_map_total).reshape(
        tenant_token_count, adapter_rank_size, hidden_units_width
    )
    adapter_output_gradient = (scaling_factor * output_map_total).reshape(
        tenant_token_count, adapter_rank_size, model_dimension_width
    )
    return (hidden_gradient, adapter_input_gradient, adapter_output_gradient)


def solution(mesh):
    in_specs = (
        P(("dp", "adapter", "fsdp")),
        P(("dp", "adapter", "fsdp"), None),
        P(("dp", "adapter", "fsdp"), None),
        P("adapter", "fsdp"),
        P("adapter", None, None),
        P("adapter", None, None),
    )
    out_specs = (
        P(("dp", "adapter", "fsdp"), None),
        P("adapter", None, None),
        P("adapter", None, None),
    )
    return jax.shard_map(
        on_device, mesh=mesh, in_specs=in_specs, out_specs=out_specs, check_vma=False
    )
```

profile of v0, /device:TPU:0, one launch (start us, length us, event | category | flops | bytes accessed | tf_op | source)
XLA Modules:
  0.0 185.1 jit_solution(1483464234489830159)
XLA Ops:
  8.0 0.0 copy-start
  8.0 0.0 copy-start.2
  8.0 0.9 convert_reduce_fusion
  9.0 0.7 multiply_add_fusion
  9.6 0.1 fusion.4
  9.8 0.7 all_to_all.71
  10.4 4.2 %all-to-all-start.2 = ((bf16[2,12,1]{1,2,0:T(2,128)(2,1)}), bf16[2,12,1]{1,2,0:T(2,128)(2,1)S(1)}, u32[]{:S(2)}, u32[]{:S(2)}) async-start(bf16[2,12,1]{1,2,0:T(2,128)(2,1)} %all_to_all.71), calls=%async_computation.3 | async-start | bytes 2048 | tf_op jit(solution)/shard_map/all_to_all | solution.py:66
  14.6 1.1 convolution_convert_fusion.3
  15.8 0.8 all_to_all.62
  16.5 1.8 all-to-all-done.2
  18.3 3.4 %all-to-all-start.3 = ((bf16[2,12,4096]{2,1,0:T(8,128)(2,1)}), bf16[2,12,4096]{2,1,0:T(8,128)(2,1)S(1)}, u32[]{:S(2)}, u32[]{:S(2)}) async-start(bf16[2,12,4096]{2,1,0:T(8,128)(2,1)} %all_to_all.62), calls=%async_computation.4 | async-start | bytes 524288 | tf_op jit(solution)/shard_map/all_to_all | solution.py:64
  21.8 0.0 copy-done.2
  21.8 0.7 copy.30
  22.5 4.5 %all-to-all-done.3 = bf16[2,12,4096]{2,1,0:T(8,128)(2,1)S(1)} async-done(((bf16[2,12,4096]{2,1,0:T(8,128)(2,1)}), bf16[2,12,4096]{2,1,0:T(8,128)(2,1)S(1)}, u32[]{:S(2)}, u32[]{:S(2)}) %all-to-all-start.3) | async-done | bytes 196640 | tf_op jit(solution)/shard_map/all_to_all | solution.py:64
  27.0 3.4 %all-to-all-start = ((bf16[24,4,1024]{2,0,1:T(8,128)(2,1)}), bf16[24,4,1024]{2,0,1:T(8,128)(2,1)S(1)}, u32[]{:S(2)}, u32[]{:S(2)}) async-start(bf16[24,4,1024]{2,0,1:T(8,128)(2,1)} %bitcast.43), calls=%async_computation | async-start | bytes 393216 | tf_op jit(solution)/shard_map/all_to_all | solution.py:29
  30.3 0.0 copy-done
  30.3 0.3 convolution_convert_fusion
  30.7 1.1 all_to_all.68
  31.8 0.0 copy-start.4
  31.8 3.8 %all-to-all-done = bf16[24,4,1024]{2,0,1:T(8,128)(2,1)S(1)} async-done(((bf16[24,4,1024]{2,0,1:T(8,128)(2,1)}), bf16[24,4,1024]{2,0,1:T(8,128)(2,1)S(1)}, u32[]{:S(2)}, u32[]{:S(2)}) %all-to-all-start) | async-done | bytes 196640 | tf_op jit(solution)/shard_map/all_to_all | solution.py:29
  35.6 3.6 %all-to-all-start.5 = ((bf16[2,12,14336]{2,1,0:T(8,128)(2,1)}), bf16[2,12,14336]{2,1,0:T(8,128)(2,1)S(1)}, u32[]{:S(2)}, u32[]{:S(2)}) async-start(bf16[2,12,14336]{2,1,0:T(8,128)(2,1)} %all_to_all.68), calls=%async_computation.6 | async-start | bytes 1835008 | tf_op jit(solution)/shard_map/all_to_all | solution.py:65
  39.2 0.0 all-reduce.3.cloned.1.call-start
  39.2 0.1 eq.45
  39.3 0.1 all_to_all.64
  39.4 0.0 copy-done.4
  39.4 0.2 fusion.2
  39.6 15.7 %all_gather.3 = bf16[192,1024]{1,0:T(8,128)(2,1)S(1)} all-gather(bf16[96,1024]{1,0:T(8,128)(2,1)S(1)} %bitcast.47), channel_id=1, replica_groups=mesh['dp'=4,'adapter'=2,'fsdp'=4] {'adapter'}, dimensions={0}, use_global_device_ids=true | all-gather | bytes 589824 | tf_op jit(solution)/shard_map/all_gather | solution.py:30
  55.3 0.0 copy-start.1
  55.3 0.0 all-to-all-done.5
  55.3 0.2 all_to_all.70
  55.5 1.1 convolution_convert_fusion.1
  56.6 0.0 copy-done.1
  56.6 1.2 convolution_convert_fusion.4
  57.8 0.0 all-reduce.3.cloned.1.call-update
  57.8 0.0 reduce-scatter.2.cloned.1.call-start
  57.9 11.7 %convolution_convert_fusion.2 = bf16[192,7168]{1,0:T(8,128)(2,1)} fusion(bf16[192,1024]{1,0:T(8,128)(2,1)S(1)} %bitcast.49, bf16[7168,1024]{1,0:T(8,128)(2,1)} %param.9), kind=kOutput, calls=%fused_computation.6 | convolution fusion | flops 2819948544 | bytes 17825792 | tf_op jit(solution)/shard_map/dot_general | solution.py:38
  69.6 0.0 reduce-scatter.2.cloned.1.call-update
  69.6 0.4 fusion
  70.0 0.2 all_to_all.65
  70.2 13.5 %all_to_all.78 = bf16[2,12,14336]{2,1,0:T(8,128)(2,1)S(1)} all-to-all(bf16[2,12,14336]{2,1,0:T(8,128)(2,1)S(1)} %all_to_all.65), channel_id=1, replica_groups=mesh['dp'=4,'adapter'=2,'fsdp'=4] {'adapter'}, dimensions={0} | all-to-all | bytes 1376256 | tf_op jit(solution)/shard_map/all_to_all | solution.py:106
  83.7 0.2 all_to_all.67
  83.9 77.5 %all-reduce.3.cloned.1.call-done = (bf16[16,14336]{1,0:T(8,128)(2,1)}, bf16[16,4096]{1,0:T(8,128)(2,1)}) async-done(((bf16[16,14336]{1,0:T(8,128)(2,1)}, bf16[16,4096]{1,0:T(8,128)(2,1)}), (bf16[16,14336]{1,0:T(8,128)(2,1)}, bf16[16,4096]{1,0:T(8,128)(2,1)})) %all-reduce.3.cloned.1.call-update) | async-done | bytes 589840 | tf_op jit(solution)/shard_map/psum | solution.py:114
  161.4 0.0 copy-start.3
  161.4 2.0 %multiply_bitcast_fusion = f32[1,16,14336]{2,1,0:T(8,128)} fusion(bf16[16,14336]{1,0:T(8,128)(2,1)} %get-tuple-element.3), kind=kLoop, calls=%fused_computation.16 | loop fusion | flops 458752 | bytes 1376256 | tf_op jit(solution)/shard_map/reshape | solution.py:117
  163.4 0.0 reduce-scatter.2.cloned.1.call-done
  163.4 3.5 %all-to-all-start.1 = ((bf16[2,24,7168]{2,1,0:T(8,128)(2,1)}), bf16[2,24,7168]{2,1,0:T(8,128)(2,1)S(1)}, u32[]{:S(2)}, u32[]{:S(2)}) async-start(bf16[2,24,7168]{2,1,0:T(8,128)(2,1)} %bitcast.48), calls=%async_computation.2 | async-start | bytes 1376256 | tf_op jit(solution)/shard_map/all_to_all | solution.py:45
  166.9 0.0 copy-done.3
  167.0 0.7 multiply_bitcast_fusion.1
  167.7 8.5 %all-to-all-done.1 = bf16[2,24,7168]{2,1,0:T(8,128)(2,1)S(1)} async-done(((bf16[2,24,7168]{2,1,0:T(8,128)(2,1)}), bf16[2,24,7168]{2,1,0:T(8,128)(2,1)S(1)}, u32[]{:S(2)}, u32[]{:S(2)}) %all-to-all-start.1) | async-done | bytes 688160 | tf_op jit(solution)/shard_map/all_to_all | solution.py:45
  176.2 0.1 convert_bitcast_fusion
  176.3 0.1 copy.28
  176.4 1.2 fusion.1
  (2 shorter events, 0.0 us)
Async XLA Ops:
  8.0 22.3 %copy-start = (bf16[24,14336]{1,0:T(8,128)(2,1)S(1)}, bf16[24,14336]{1,0:T(8,128)(2,1)}, u32[]{:S(2)}) copy-start(bf16[24,14336]{1,0:T(8,128)(2,1)} %param.8) | copy-start | bytes 2064388
  8.0 13.8 %copy-start.2 = (bf16[24,4096]{1,0:T(8,128)(2,1)S(1)}, bf16[24,4096]{1,0:T(8,128)(2,1)}, u32[]{:S(2)}) copy-start(bf16[24,4096]{1,0:T(8,128)(2,1)} %param.7) | copy-start | bytes 589828
  10.4 7.9 %all-to-all-start.2 = ((bf16[2,12,1]{1,2,0:T(2,128)(2,1)}), bf16[2,12,1]{1,2,0:T(2,128)(2,1)S(1)}, u32[]{:S(2)}, u32[]{:S(2)}) async-start(bf16[2,12,1]{1,2,0:T(2,128)(2,1)} %all_to_all.71), calls=%async_computation.3 | async-start | bytes 2048 | tf_op jit(solution)/shard_map/all_to_all | solution.py:66
  18.3 8.6 %all-to-all-start.3 = ((bf16[2,12,4096]{2,1,0:T(8,128)(2,1)}), bf16[2,12,4096]{2,1,0:T(8,128)(2,1)S(1)}, u32[]{:S(2)}, u32[]{:S(2)}) async-start(bf16[2,12,4096]{2,1,0:T(8,128)(2,1)} %all_to_all.62), calls=%async_computation.4 | async-start | bytes 524288 | tf_op jit(solution)/shard_map/all_to_all | solution.py:64
  27.0 8.6 %all-to-all-start = ((bf16[24,4,1024]{2,0,1:T(8,128)(2,1)}), bf16[24,4,1024]{2,0,1:T(8,128)(2,1)S(1)}, u32[]{:S(2)}, u32[]{:S(2)}) async-start(bf16[24,4,1024]{2,0,1:T(8,128)(2,1)} %bitcast.43), calls=%async_computation | async-start | bytes 393216 | tf_op jit(solution)/shard_map/all_to_all | solution.py:29
  31.8 7.6 %copy-start.4 = (bf16[1,16,4096]{2,1,0:T(8,128)(2,1)S(1)}, bf16[1,16,4096]{2,1,0:T(8,128)(2,1)}, u32[]{:S(2)}) copy-start(bf16[1,16,4096]{2,1,0:T(8,128)(2,1)} %param.11) | copy-start | bytes 393220
  35.6 19.7 %all-to-all-start.5 = ((bf16[2,12,14336]{2,1,0:T(8,128)(2,1)}), bf16[2,12,14336]{2,1,0:T(8,128)(2,1)S(1)}, u32[]{:S(2)}, u32[]{:S(2)}) async-start(bf16[2,12,14336]{2,1,0:T(8,128)(2,1)} %all_to_all.68), calls=%async_computation.6 | async-start | bytes 1835008 | tf_op jit(solution)/shard_map/all_to_all | solution.py:65
  39.2 122.2 %all-reduce.3.cloned.1.call-start = ((), (), s32[]{:S(2)}) async-start(), calls=%async_computation.8 | async-start | bytes 1179648 | tf_op jit(solution)/shard_map/psum | solution.py:114
  55.3 1.3 copy-start.1
  57.8 105.6 %reduce-scatter.2.cloned.1.call-start = ((), (), s32[]{:S(2)}) async-start(), calls=%async_computation.7 | async-start | bytes 3440640 | tf_op jit(solution)/shard_map/reduce_scatter | solution.py:37
  161.4 5.6 %copy-start.3 = (bf16[16,4096]{1,0:T(8,128)(2,1)S(1)}, bf16[16,4096]{1,0:T(8,128)(2,1)}, u32[]{:S(2)}) copy-start(bf16[16,4096]{1,0:T(8,128)(2,1)} %get-tuple-element.4) | copy-start | bytes 393220
  163.4 12.8 %all-to-all-start.1 = ((bf16[2,24,7168]{2,1,0:T(8,128)(2,1)}), bf16[2,24,7168]{2,1,0:T(8,128)(2,1)S(1)}, u32[]{:S(2)}, u32[]{:S(2)}) async-start(bf16[2,24,7168]{2,1,0:T(8,128)(2,1)} %bitcast.48), calls=%async_computation.2 | async-start | bytes 1376256 | tf_op jit(solution)/shard_map/all_to_all | solution.py:45
Sparse Core Ops, SparseCore 0:
  58.0 103.3 all-reduce.2
Sparse Core Ops, SparseCore 1:
  69.7 35.7 reduce-scatter.1
where the time goes:
time: 186 us; the launch traced here: 185 us
  waiting for transfers between devices  96.1 us (52%)
  blocking collectives  29.2 us (16%)
  starting transfers between devices  18.2 us (10%)
  matrix products  17.3 us (9%)
  between operations  15.6 us (8%)
  other arithmetic  4.49 us (2%)
  local copies, waits for them, and re-layouts  4.02 us (2%)
    psum x1, waiting for transfers between devices, on_device(): lax.psum(grad_a_part.astype(jnp.bfloat16), ('dp', 'fsdp'))  77.5 us
    all_gather x1, blocking collectives, on_device(): spread = lax.all_gather(own_columns, 'adapter', axis=0, tiled=True)  15.7 us
    all_to_all x1, blocking collectives, on_device(): lax.all_to_all(adapter_token_rows, 'adapter', split_axis=0, concat_axis=0...  13.5 us
    dot_general x1, matrix products, on_device(): lax.dot_general(taken, frozen_down_weight, (((1,), (1,)), ((), ())), pref...  11.7 us
    all_to_all x1, waiting for transfers between devices, on_device(): lax.all_to_all(partial_base, 'adapter', split_axis=0, concat_axis=1, tile...  8.49 us
    all_to_all x1, waiting for transfers between devices, on_device(): lax.all_to_all(send_out, 'adapter', split_axis=0, concat_axis=0, tiled=True)  4.46 us
    all_to_all x1, starting transfers between devices, on_device(): lax.all_to_all(send_tag, 'adapter', split_axis=0, concat_axis=0, tiled=True)  4.23 us
    all_to_all x1, waiting for transfers between devices, on_device(): lax.all_to_all(output_gradient, 'fsdp', split_axis=1, concat_axis=0, tile...  3.82 us
  transfers between devices with their start and end apart: 7, of which 5 were waited for; matrix products, arithmetic and copies ran while one was open for 9% of the time, Pallas kernels for 0%

commit v1 on v0

--- a/solution.py
+++ b/solution.py
@@ -1,6 +1,10 @@
+import functools
+
 import jax
 import jax.numpy as jnp
 from jax import lax
+from jax.experimental import pallas as pl
+from jax.experimental.pallas import tpu as pltpu
 from jax.sharding import PartitionSpec as P
 
 adapter_scale = 2.0
@@ -123,6 +127,389 @@
     return (hidden_gradient, adapter_input_gradient, adapter_output_gradient)
 
 
+def chunk_count(width):
+    for count in (7, 8, 4, 2):
+        if width % (count * 128) == 0:
+            return count
+    return 1
+
+
+def fused_kernel(
+    scale, chunks, idx_ref, og_ref, hid_ref, w_ref, a_ref, b_ref,
+    out_ref, ga_ref, gb_ref,
+    wv, xrec, xs, keep, psend, prec, ysend, yrec, xsend, xrecv,
+    aoth, both,
+    gsend_a, gkeep_a, grec_a, zs_a, zrec_a, sum_a, xg_a, xgrec_a, yg_a, ygrec_a, full_a,
+    gsend_b, gkeep_b, grec_b, zs_b, zrec_b, sum_b, xg_b, xgrec_b, yg_b, ygrec_b, full_b,
+    wsem, ssem, rsem, csend, crecv,
+):
+    f32, bf16 = jnp.float32, jnp.bfloat16
+    d, a, f = lax.axis_index("dp"), lax.axis_index("adapter"), lax.axis_index("fsdp")
+    groups = lax.axis_size("dp")
+    c = lax.rem(f, 2)
+    y = f // 2
+    toks = og_ref.shape[0]
+    half = w_ref.shape[0]
+    slab = w_ref.shape[1]
+    ch = half // chunks
+    hidden_width = hid_ref.shape[1]
+    model_width = og_ref.shape[1]
+    fc = 2 * y + (1 - c)
+    fy = 2 * (1 - y) + c
+    core, ynb, xnb = (d, a, fc), (d, a, fy), (d, 1 - a, f)
+
+    def plane(yr, cr, ar):
+        yy = (1 - y) if yr else y
+        cc = (1 - c) if cr else c
+        return (d, (1 - a) if ar else a, 2 * yy + cc)
+
+    peers = [(yr, cr, ar) for yr in (1, 0) for cr in (0, 1) for ar in (0, 1) if yr or cr or ar]
+
+    def zdev(r):
+        return (lax.rem(d + r, groups), a, f)
+
+    counter = [0]
+
+    def remote(src, dst, dev):
+        k = counter[0]
+        counter[0] += 1
+        return pltpu.make_async_remote_copy(
+            src_ref=src, dst_ref=dst, send_sem=ssem.at[k], recv_sem=rsem.at[k],
+            device_id=dev, device_id_type=pl.DeviceIdType.MESH,
+        )
+
+    started = []
+
+    def go(copy):
+        copy.start()
+        started.append(copy)
+        return copy
+
+    def cols(start, width, align):
+        return pl.ds(pl.multiple_of(start, align), width)
+
+    def w_copy(j):
+        return pltpu.make_async_copy(
+            w_ref.at[pl.ds(pl.multiple_of(j * ch, ch), ch), :], wv.at[j], wsem.at[j]
+        )
+
+    for j in range(chunks):
+        w_copy(j).start()
+
+    barrier = pltpu.get_barrier_semaphore()
+    all_peers = [plane(*p) for p in peers] + [zdev(r) for r in range(1, groups)]
+    for dev in all_peers:
+        pl.semaphore_signal(barrier, inc=1, device_id=dev, device_id_type=pl.DeviceIdType.MESH)
+    pl.semaphore_wait(barrier, len(all_peers))
+
+    hb = model_width // 2
+    ha = hidden_width // 2
+    bcols = cols(c * hb, hb, hb)
+    acols = cols(c * ha, ha, ha)
+    bx = go(remote(b_ref.at[0, :, bcols], both.at[:, bcols], xnb))
+    ogc = []
+    for p in peers:
+        dev = plane(*p)
+        ogc.append(
+            go(remote(og_ref.at[:, cols(dev[2] * slab, slab, slab)], xrec.at[p[0], p[1], p[2]], dev))
+        )
+    ax = go(remote(a_ref.at[0, :, acols], aoth.at[:, acols], xnb))
+    bx.wait_recv()
+    bp = go(remote(both.at[:, bcols], both.at[:, bcols], core))
+
+    def nt(lhs, rhs):
+        return lax.dot_general(lhs, rhs, (((1,), (1,)), ((), ())), preferred_element_type=f32)
+
+    own_mask = (idx_ref[...] == a).astype(f32)
+    oth_mask = (idx_ref[...] == 1 - a).astype(f32)
+
+    def masked_pair(lhs, own, oth):
+        return jnp.concatenate(
+            [nt(lhs, own) * own_mask, nt(lhs, oth) * oth_mask], axis=1
+        )
+
+    def grad_first(left_t, ref, gsend, gkeep, grec, width):
+        gsend[...] = jnp.dot(
+            left_t, ref[:, cols((1 - c) * width, width, width)], preferred_element_type=f32
+        ).astype(bf16)
+        copy = go(remote(gsend, grec, core))
+        gkeep[...] = jnp.dot(
+            left_t, ref[:, cols(c * width, width, width)], preferred_element_type=f32
+        )
+        return copy
+
+    def grad_z(copy, gkeep, grec, zs, zrec):
+        copy.wait_recv()
+        wq = zs.shape[2]
+        for q in range(groups):
+            zs[q] = (
+                gkeep[:, q * wq : (q + 1) * wq] + grec[:, q * wq : (q + 1) * wq].astype(f32)
+            ).astype(bf16)
+        return [
+            go(remote(zs.at[lax.rem(d + r, groups)], zrec.at[r - 1], zdev(r)))
+            for r in range(1, groups)
+        ]
+
+    def grad_x(copies, zs, zrec, acc, xg, xgrec):
+        for copy in copies:
+            copy.wait_recv()
+        total = zs[d].astype(f32)
+        for r in range(groups - 1):
+            total = total + zrec[r].astype(f32)
+        rank = total.shape[0] // 2
+        acc[...] = total[:rank]
+        xg[...] = total[rank:].astype(bf16)
+        return go(remote(xg, xgrec, xnb))
+
+    def grad_y(copy, acc, xgrec, yg, ygrec):
+        copy.wait_recv()
+        yg[...] = (acc[...] + xgrec[...].astype(f32)).astype(bf16)
+        return go(remote(yg, ygrec, ynb))
+
+    def grad_gather(copy, yg, ygrec, full):
+        copy.wait_recv()
+        full[c, d] = (yg[...].astype(f32) + ygrec[...].astype(f32)).astype(bf16)
+        return [
+            go(remote(full.at[c, d], full.at[c, d], zdev(r))) for r in range(1, groups)
+        ]
+
+    def grad_core(copies, full):
+        for copy in copies:
+            copy.wait_recv()
+        return go(remote(full.at[c], full.at[c], core))
+
+    def grad_out(copy, full, ref):
+        copy.wait_recv()
+        wq = full.shape[3]
+        for h in range(2):
+            for q in range(groups):
+                at = (h * groups + q) * wq
+                ref[0, :, at : at + wq] = scale * full[h, q].astype(f32)
+
+    bp.wait_recv()
+    og = og_ref[...]
+    coef = masked_pair(og, b_ref[0], both[...])
+    coef_t = jnp.transpose(coef, (1, 0)).astype(bf16)
+    rank = coef.shape[1] // 2
+    coef_own = coef[:, :rank].astype(bf16)
+    coef_oth = coef[:, rank:].astype(bf16)
+    ga1 = grad_first(coef_t, hid_ref, gsend_a, gkeep_a, grec_a, ha)
+
+    for copy in ogc:
+        copy.wait_recv()
+    at = 0
+    for yr in (0, 1):
+        for cr in (0, 1):
+            rows = []
+            for ar in (0, 1):
+                if yr or cr or ar:
+                    rows.append(xrec[yr, cr, ar].astype(f32))
+                else:
+                    rows.append(og_ref[:, cols(f * slab, slab, slab)].astype(f32))
+            pair = jnp.concatenate(rows, axis=0).astype(bf16)
+            xs[at : at + 2 * toks] = pair
+            at += 2 * toks
+
+    def chunk_copy(k, src, dst, dev, j):
+        return pltpu.make_async_remote_copy(
+            src_ref=src.at[j], dst_ref=dst.at[j], send_sem=csend.at[k, j],
+            recv_sem=crecv.at[k, j], device_id=dev, device_id_type=pl.DeviceIdType.MESH,
+        )
+
+    def core_copy(j):
+        return chunk_copy(0, psend, prec, core, j)
+
+    def y_copy(j):
+        return chunk_copy(1, ysend, yrec, ynb, j)
+
+    def x_copy(j):
+        return chunk_copy(2, xsend, xrecv, xnb, j)
+
+    pair_rows = 2 * toks
+
+    def stage_matmul(j):
+        w_copy(j).wait()
+        part = nt(xs[...], wv[j])
+        for yr in (0, 1):
+            at = 2 * yr * pair_rows
+            keep[j, yr] = part[at : at + pair_rows]
+            psend[j, yr] = part[at + pair_rows : at + 2 * pair_rows].astype(bf16)
+        core_copy(j).start()
+
+    def stage_y(j):
+        core_copy(j).wait_recv()
+        ysend[j] = (keep[j, 1] + prec[j, 1].astype(f32)).astype(bf16)
+        y_copy(j).start()
+
+    def lora(at):
+        own = jnp.dot(coef_own, a_ref[0, :, at], preferred_element_type=f32)
+        oth = jnp.dot(coef_oth, aoth[:, at], preferred_element_type=f32)
+        return (adapter_scale * (own + oth)).astype(bf16).astype(f32)
+
+    def stage_x(j):
+        y_copy(j).wait_recv()
+        total = keep[j, 0] + prec[j, 0].astype(f32) + yrec[j].astype(f32)
+        xsend[j] = total[toks:].astype(bf16)
+        x_copy(j).start()
+        at = cols(a * half + j * ch, ch, ch)
+        own = total[:toks].astype(bf16).astype(f32)
+        out_ref[:, at] = (own + lora(at)).astype(bf16)
+
+    def stage_out(j):
+        x_copy(j).wait_recv()
+        at = cols((1 - a) * half + j * ch, ch, ch)
+        out_ref[:, at] = (xrecv[j].astype(f32) + lora(at)).astype(bf16)
+
+    def loop(first, last):
+        @pl.loop(first, last)
+        def _(j):
+            stage_matmul(j)
+            stage_y(j - 1)
+
+    mid = min(chunks, 1 + chunks // 2)
+    stage_matmul(0)
+    loop(1, mid)
+    ga2 = grad_z(ga1, gkeep_a, grec_a, zs_a, zrec_a)
+    ax.wait_recv()
+    ap = go(remote(aoth.at[:, acols], aoth.at[:, acols], core))
+    loop(mid, chunks)
+    stage_y(chunks - 1)
+    ap.wait_recv()
+    low = masked_pair(hid_ref[...], a_ref[0], aoth[...])
+    low_t = jnp.transpose(low, (1, 0)).astype(bf16)
+    gb1 = grad_first(low_t, og_ref, gsend_b, gkeep_b, grec_b, hb)
+
+    state = {}
+
+    def s_gb2():
+        state["gb2"] = grad_z(gb1, gkeep_b, grec_b, zs_b, zrec_b)
+
+    def s_ga3():
+        state["ga3"] = grad_x(ga2, zs_a, zrec_a, sum_a, xg_a, xgrec_a)
+
+    def s_ga4():
+        state["ga4"] = grad_y(state["ga3"], sum_a, xgrec_a, yg_a, ygrec_a)
+
+    def s_gb3():
+        state["gb3"] = grad_x(state["gb2"], zs_b, zrec_b, sum_b, xg_b, xgrec_b)
+
+    def s_ga5():
+        state["ga5"] = grad_gather(state["ga4"], yg_a, ygrec_a, full_a)
+
+    def s_gb4():
+        state["gb4"] = grad_y(state["gb3"], sum_b, xgrec_b, yg_b, ygrec_b)
+
+    def s_gb5():
+        state["gb5"] = grad_gather(state["gb4"], yg_b, ygrec_b, full_b)
+
+    def s_ga6():
+        state["ga6"] = grad_core(state["ga5"], full_a)
+
+    def s_gb6():
+        state["gb6"] = grad_core(state["gb5"], full_b)
+
+    between = [[s_gb2], [s_ga3], [s_ga4, s_gb3], [s_gb4, s_ga5], [s_gb5], [s_ga6], [s_gb6]]
+    for j in range(max(chunks, len(between))):
+        if j < chunks:
+            stage_x(j)
+        if j < len(between):
+            for step in between[j]:
+                step()
+    for j in range(chunks):
+        stage_out(j)
+    grad_out(state["ga6"], full_a, ga_ref)
+    grad_out(state["gb6"], full_b, gb_ref)
+    for copy in started:
+        copy.wait_send()
+    for j in range(chunks):
+        core_copy(j).wait_send()
+        y_copy(j).wait_send()
+        x_copy(j).wait_send()
+
+
+def fused_on_device(
+    adapter_index, output_gradient, hidden, frozen_down_weight, adapter_input_maps,
+    adapter_output_maps,
+):
+    toks, model_width = output_gradient.shape
+    hidden_width = hidden.shape[1]
+    half, slab = frozen_down_weight.shape
+    rank = adapter_input_maps.shape[1]
+    groups = lax.axis_size("dp")
+    devices = groups * lax.axis_size("adapter") * lax.axis_size("fsdp")
+    scale = adapter_scale * lax.axis_size("adapter") / (toks * devices)
+    chunks = chunk_count(half)
+    ch = half // chunks
+    f32, bf16 = jnp.float32, jnp.bfloat16
+
+    def grad_scratch(width):
+        wh = width // 2
+        wq = wh // groups
+        return [
+            pltpu.VMEM((2 * rank, wh), bf16),
+            pltpu.VMEM((2 * rank, wh), f32),
+            pltpu.VMEM((2 * rank, wh), bf16),
+            pltpu.VMEM((groups, 2 * rank, wq), bf16),
+            pltpu.VMEM((groups - 1, 2 * rank, wq), bf16),
+            pltpu.VMEM((rank, wq), f32),
+            pltpu.VMEM((rank, wq), bf16),
+            pltpu.VMEM((rank, wq), bf16),
+            pltpu.VMEM((rank, wq), bf16),
+            pltpu.VMEM((rank, wq), bf16),
+            pltpu.VMEM((2, groups, rank, wq), bf16),
+        ]
+
+    copies = 4 + 7 + 2 * (4 + 2 * (groups - 1))
+    vmem = pl.BlockSpec(memory_space=pltpu.VMEM)
+    return pl.pallas_call(
+        functools.partial(fused_kernel, scale, chunks),
+        out_shape=(
+            jax.ShapeDtypeStruct((toks, hidden_width), bf16),
+            jax.ShapeDtypeStruct((1, rank, hidden_width), f32),
+            jax.ShapeDtypeStruct((1, rank, model_width), f32),
+        ),
+        in_specs=[vmem, vmem, vmem, pl.BlockSpec(memory_space=pl.ANY), vmem, vmem],
+        out_specs=(vmem, vmem, vmem),
+        scratch_shapes=[
+            pltpu.VMEM((chunks, ch, slab), bf16),
+            pltpu.VMEM((2, 2, 2, toks, slab), bf16),
+            pltpu.VMEM((8 * toks, slab), bf16),
+            pltpu.VMEM((chunks, 2, 2 * toks, ch), f32),
+            pltpu.VMEM((chunks, 2, 2 * toks, ch), bf16),
+            pltpu.VMEM((chunks, 2, 2 * toks, ch), bf16),
+            pltpu.VMEM((chunks, 2 * toks, ch), bf16),
+            pltpu.VMEM((chunks, 2 * toks, ch), bf16),
+            pltpu.VMEM((chunks, toks, ch), bf16),
+            pltpu.VMEM((chunks, toks, ch), bf16),
+            pltpu.VMEM((rank, hidden_width), bf16),
+            pltpu.VMEM((rank, model_width), bf16),
+            *grad_scratch(hidden_width),
+            *grad_scratch(model_width),
+            pltpu.SemaphoreType.DMA((chunks,)),
+            pltpu.SemaphoreType.DMA((copies,)),
+            pltpu.SemaphoreType.DMA((copies,)),
+            pltpu.SemaphoreType.DMA((3, chunks)),
+            pltpu.SemaphoreType.DMA((3, chunks)),
+        ],
+        compiler_params=pltpu.CompilerParams(collective_id=0, has_side_effects=True),
+    )(
+        adapter_index.reshape(toks, 1), output_gradient, hidden, frozen_down_weight,
+        adapter_input_maps, adapter_output_maps,
+    )
+
+
+def per_device(mesh):
+    def body(*args):
+        fused = (
+            mesh.shape["adapter"] == 2
+            and mesh.shape["fsdp"] == 4
+            and args[4].shape[0] == 1
+        )
+        return fused_on_device(*args) if fused else on_device(*args)
+
+    return body
+
+
 def solution(mesh):
     in_specs = (
         P(("dp", "adapter", "fsdp")),
@@ -138,5 +525,5 @@
         P("adapter", None, None),
     )
     return jax.shard_map(
-        on_device, mesh=mesh, in_specs=in_specs, out_specs=out_specs, check_vma=False
-    )
+        per_device(mesh), mesh=mesh, in_specs=in_specs, out_specs=out_specs, check_vma=False
+    )

time: 186 us -> 57.5 us (0.31)
  waiting for transfers between devices: 96.1 us -> 0 us
  Pallas kernels: 0 us -> 49.5 us
  blocking collectives: 29.2 us -> 0 us
  starting transfers between devices: 18.2 us -> 0 us
  matrix products: 17.3 us -> 0 us
  between operations: 15.6 us -> 0.64 us
  other arithmetic: 4.49 us -> 0 us
  local copies, waits for them, and re-layouts: 4.02 us -> 7.15 us
    psum x1 -> x0, waiting for transfers between devices: 77.5 us -> none  [on_device(): lax.psum(grad_a_part.astype(jnp.bfloat16), ('dp', 'fsdp'))]
    pallas_call x0 -> x1, Pallas kernels: none -> 49.5 us  [fused_on_device(): pl.pallas_call(functools.partial(fused_kernel, scale, chunks), out_shape=...]
    all_to_all x5 -> x0, waiting for transfers between devices: 18.6 us -> none  [the longest x1 8.49 us: on_device(): lax.all_to_all(partial_base, 'adapter', split_axis=0, concat_axis=1, tile...]
    all_to_all x5 -> x0, starting transfers between devices: 18.1 us -> none  [the longest x1 4.23 us: on_device(): lax.all_to_all(send_tag, 'adapter', split_axis=0, concat_axis=0, tiled=True)]
    dot_general x9 -> x0, matrix products: 17.3 us -> none  [the longest x1 11.7 us: on_device(): lax.dot_general(taken, frozen_down_weight, (((1,), (1,)), ((), ())), pref...]
    all_gather x1 -> x0, blocking collectives: 15.7 us -> none  [on_device(): spread = lax.all_gather(own_columns, 'adapter', axis=0, tiled=True)]
    all_to_all x1 -> x0, blocking collectives: 13.5 us -> none  [on_device(): lax.all_to_all(adapter_token_rows, 'adapter', split_axis=0, concat_axis=0...]
    unnamed x10 -> x3, local copies, waits for them, and re-layouts: 0.03 us -> 5.82 us
  transfers between devices with their start and end apart: 7 -> 0, of which waited for: 5 -> 0; matrix products, arithmetic and copies ran while one was open for 9% -> 0% of each run, Pallas kernels for 0% -> 0%
where the time goes in v1:
time: 57.5 us; the launch traced here: 57.3 us
  Pallas kernels  49.5 us (86%)
  local copies, waits for them, and re-layouts  7.15 us (12%)
  between operations  0.64 us (1%)
    pallas_call x1, Pallas kernels, fused_on_device(): pl.pallas_call(functools.partial(fused_kernel, scale, chunks), out_shape=...  49.5 us
    unnamed x3, local copies, waits for them, and re-layouts  5.82 us
    reshape x1, local copies, waits for them, and re-layouts, fused_on_device(): adapter_index.reshape(toks, 1)  1.33 us

profile of v1, /device:TPU:0, one launch (start us, length us, event | category | flops | bytes accessed | tf_op | source)
XLA Modules:
  0.0 57.3 jit_solution(6756063911095157737)
XLA Ops:
  0.6 1.3 %copy.9.idx_ref = s32[24,1]{1,0:T(8,128)} copy(s32[24,1]{0,1:T(1,128)} %bitcast.1) | data formatting | bytes 192 | tf_op jit(solution)/shard_map/reshape | solution.py:496
  2.0 49.5 %shard_map.85 = (bf16[24,14336]{1,0:T(8,128)(2,1)}, f32[1,16,14336]{2,1,0:T(8,128)}, f32[1,16,4096]{2,1,0:T(8,128)}) custom-call(s32[24,1]{1,0:T(8,128)} %copy.9.idx_ref, bf16[24,4096]{1,0:T(8,128)(2,1)} %og_ref.1, bf16[24,14336]{1,0:T(8,128)(2,1)} %hid_ref.1, bf16[7168,1024]{1,0:T(8,128)(2,1)} %w_ref.1, bf16[1,16,14336]{2,1,0:T(8,128)(2,1)} %a_ref.1, ...), custom_call_target="tpu_custom_call" | custom-call | tf_op jit(solution)/shard_map/pallas_call | solution.py:464
  51.4 2.0 %copy.13 = bf16[24,14336]{1,0:T(8,128)(2,1)} copy(bf16[24,14336]{1,0:T(8,128)(2,1)} %get-tuple-element.6) | data formatting | bytes 1376256
  53.4 2.2 %copy.14 = f32[1,16,14336]{2,1,0:T(8,128)} copy(f32[1,16,14336]{2,1,0:T(8,128)} %get-tuple-element.7) | data formatting | bytes 1835008
  55.6 1.7 %copy.15 = f32[1,16,4096]{2,1,0:T(8,128)} copy(f32[1,16,4096]{2,1,0:T(8,128)} %get-tuple-element.8) | data formatting | bytes 524288

commit v2 on v1

--- a/solution.py
+++ b/solution.py
@@ -135,13 +135,13 @@
 
 
 def fused_kernel(
-    scale, chunks, idx_ref, og_ref, hid_ref, w_ref, a_ref, b_ref,
+    chunks, idx_ref, og_hbm, hid_hbm, w_ref, a_hbm, b_hbm,
     out_ref, ga_ref, gb_ref,
-    wv, xrec, xs, keep, psend, prec, ysend, yrec, xsend, xrecv,
+    og_ref, hid_ref, a_ref, b_ref, wv, xrec, xs, keep, psend, prec, ysend, yrec, xsend, xrecv,
     aoth, both,
     gsend_a, gkeep_a, grec_a, zs_a, zrec_a, sum_a, xg_a, xgrec_a, yg_a, ygrec_a, full_a,
     gsend_b, gkeep_b, grec_b, zs_b, zrec_b, sum_b, xg_b, xgrec_b, yg_b, ygrec_b, full_b,
-    wsem, ssem, rsem, csend, crecv,
+    lsem, wsem, ssem, rsem, csend, crecv,
 ):
     f32, bf16 = jnp.float32, jnp.bfloat16
     d, a, f = lax.axis_index("dp"), lax.axis_index("adapter"), lax.axis_index("fsdp")
@@ -193,7 +193,18 @@
             w_ref.at[pl.ds(pl.multiple_of(j * ch, ch), ch), :], wv.at[j], wsem.at[j]
         )
 
-    for j in range(chunks):
+    local = [
+        pltpu.make_async_copy(src, dst, lsem.at[k])
+        for k, (src, dst) in enumerate(
+            ((og_hbm, og_ref), (b_hbm, b_ref), (hid_hbm, hid_ref), (a_hbm, a_ref))
+        )
+    ]
+    local[0].start()
+    w_copy(0).start()
+    w_copy(1).start()
+    for copy in local[1:]:
+        copy.start()
+    for j in range(2, chunks):
         w_copy(j).start()
 
     barrier = pltpu.get_barrier_semaphore()
@@ -206,16 +217,14 @@
     ha = hidden_width // 2
     bcols = cols(c * hb, hb, hb)
     acols = cols(c * ha, ha, ha)
-    bx = go(remote(b_ref.at[0, :, bcols], both.at[:, bcols], xnb))
+    bx = go(remote(b_hbm.at[0, :, bcols], both.at[:, bcols], xnb))
     ogc = []
     for p in peers:
         dev = plane(*p)
         ogc.append(
-            go(remote(og_ref.at[:, cols(dev[2] * slab, slab, slab)], xrec.at[p[0], p[1], p[2]], dev))
-        )
-    ax = go(remote(a_ref.at[0, :, acols], aoth.at[:, acols], xnb))
-    bx.wait_recv()
-    bp = go(remote(both.at[:, bcols], both.at[:, bcols], core))
+            go(remote(og_hbm.at[:, cols(dev[2] * slab, slab, slab)], xrec.at[p[0], p[1], p[2]], dev))
+        )
+    ax = go(remote(a_hbm.at[0, :, acols], aoth.at[:, acols], xnb))
 
     def nt(lhs, rhs):
         return lax.dot_general(lhs, rhs, (((1,), (1,)), ((), ())), preferred_element_type=f32)
@@ -223,10 +232,8 @@
     own_mask = (idx_ref[...] == a).astype(f32)
     oth_mask = (idx_ref[...] == 1 - a).astype(f32)
 
-    def masked_pair(lhs, own, oth):
-        return jnp.concatenate(
-            [nt(lhs, own) * own_mask, nt(lhs, oth) * oth_mask], axis=1
-        )
+    def masked_pair(own, oth, rhs):
+        return jnp.concatenate([nt(own, rhs) * own_mask, nt(oth, rhs) * oth_mask], axis=0)
 
     def grad_first(left_t, ref, gsend, gkeep, grec, width):
         gsend[...] = jnp.dot(
@@ -269,31 +276,133 @@
     def grad_gather(copy, yg, ygrec, full):
         copy.wait_recv()
         full[c, d] = (yg[...].astype(f32) + ygrec[...].astype(f32)).astype(bf16)
-        return [
+        out = [
             go(remote(full.at[c, d], full.at[c, d], zdev(r))) for r in range(1, groups)
         ]
-
-    def grad_core(copies, full):
+        return out, [go(remote(full.at[c, d], full.at[c, d], core))]
+
+    def grad_core(state, full):
+        copies, sent = state
+        for r, copy in enumerate(copies, 1):
+            copy.wait_recv()
+            at = lax.rem(d + groups - r, groups)
+            sent.append(go(remote(full.at[c, at], full.at[c, at], core)))
+        return sent
+
+    def grad_out(copies, full, ref):
         for copy in copies:
             copy.wait_recv()
-        return go(remote(full.at[c], full.at[c], core))
-
-    def grad_out(copy, full, ref):
-        copy.wait_recv()
-        wq = full.shape[3]
-        for h in range(2):
-            for q in range(groups):
-                at = (h * groups + q) * wq
-                ref[0, :, at : at + wq] = scale * full[h, q].astype(f32)
-
-    bp.wait_recv()
-    og = og_ref[...]
-    coef = masked_pair(og, b_ref[0], both[...])
-    coef_t = jnp.transpose(coef, (1, 0)).astype(bf16)
-    rank = coef.shape[1] // 2
-    coef_own = coef[:, :rank].astype(bf16)
-    coef_oth = coef[:, rank:].astype(bf16)
-    ga1 = grad_first(coef_t, hid_ref, gsend_a, gkeep_a, grec_a, ha)
+        ref[...] = full[...]
+
+    def chunk_copy(k, src, dst, dev, j):
+        return pltpu.make_async_remote_copy(
+            src_ref=src.at[j], dst_ref=dst.at[j], send_sem=csend.at[k, j],
+            recv_sem=crecv.at[k, j], device_id=dev, device_id_type=pl.DeviceIdType.MESH,
+        )
+
+    def core_copy(j):
+        return chunk_copy(0, psend, prec, core, j)
+
+    def y_copy(j):
+        return chunk_copy(1, ysend, yrec, ynb, j)
+
+    def x_copy(j):
+        return chunk_copy(2, xsend, xrecv, xnb, j)
+
+    pair_rows = 2 * toks
+
+    def stage_matmul(j):
+        w_copy(j).wait()
+        part = nt(xs[...], wv[j])
+        for yr in (0, 1):
+            at = 2 * yr * pair_rows
+            keep[j, yr] = part[at : at + pair_rows]
+            psend[j, yr] = part[at + pair_rows : at + 2 * pair_rows].astype(bf16)
+        core_copy(j).start()
+
+    def stage_y(j):
+        core_copy(j).wait_recv()
+        ysend[j] = (keep[j, 1] + prec[j, 1].astype(f32)).astype(bf16)
+        y_copy(j).start()
+
+    def lora(at):
+        coef_own, coef_oth = state["coef"]
+        own = jnp.dot(coef_own, a_ref[0, :, at], preferred_element_type=f32)
+        oth = jnp.dot(coef_oth, aoth[:, at], preferred_element_type=f32)
+        return (adapter_scale * (own + oth)).astype(bf16).astype(f32)
+
+    def stage_x(j):
+        y_copy(j).wait_recv()
+        total = keep[j, 0] + prec[j, 0].astype(f32) + yrec[j].astype(f32)
+        xsend[j] = total[toks:].astype(bf16)
+        x_copy(j).start()
+        at = cols(a * half + j * ch, ch, ch)
+        own = total[:toks].astype(bf16).astype(f32)
+        out_ref[:, at] = (own + lora(at)).astype(bf16)
+
+    def stage_out(j):
+        x_copy(j).wait_recv()
+        at = cols((1 - a) * half + j * ch, ch, ch)
+        out_ref[:, at] = (xrecv[j].astype(f32) + lora(at)).astype(bf16)
+
+    state = {}
+
+    def s_b():
+        bx.wait_recv()
+        state["bp"] = go(remote(both.at[:, bcols], both.at[:, bcols], core))
+
+    def s_coef():
+        for copy in local[:3]:
+            copy.wait()
+        state["bp"].wait_recv()
+        coef_t = masked_pair(b_ref[0], both[...], og_ref[...])
+        coef = jnp.transpose(coef_t, (1, 0)).astype(bf16)
+        rank = coef.shape[1] // 2
+        state["coef"] = (coef[:, :rank], coef[:, rank:])
+        state["ga1"] = grad_first(coef_t.astype(bf16), hid_ref, gsend_a, gkeep_a, grec_a, ha)
+
+    def s_ga2():
+        state["ga2"] = grad_z(state["ga1"], gkeep_a, grec_a, zs_a, zrec_a)
+
+    def s_a():
+        ax.wait_recv()
+        state["ap"] = go(remote(aoth.at[:, acols], aoth.at[:, acols], core))
+
+    def s_low():
+        local[3].wait()
+        state["ap"].wait_recv()
+        low_t = masked_pair(a_ref[0], aoth[...], hid_ref[...]).astype(bf16)
+        state["gb1"] = grad_first(low_t, og_ref, gsend_b, gkeep_b, grec_b, hb)
+
+    def s_gb2():
+        state["gb2"] = grad_z(state["gb1"], gkeep_b, grec_b, zs_b, zrec_b)
+
+    def s_ga3():
+        state["ga3"] = grad_x(state["ga2"], zs_a, zrec_a, sum_a, xg_a, xgrec_a)
+
+    def s_ga4():
+        state["ga4"] = grad_y(state["ga3"], sum_a, xgrec_a, yg_a, ygrec_a)
+
+    def s_gb3():
+        state["gb3"] = grad_x(state["gb2"], zs_b, zrec_b, sum_b, xg_b, xgrec_b)
+
+    def s_ga5():
+        state["ga5"] = grad_gather(state["ga4"], yg_a, ygrec_a, full_a)
+
+    def s_gb4():
+        state["gb4"] = grad_y(state["gb3"], sum_b, xgrec_b, yg_b, ygrec_b)
+
+    def s_gb5():
+        state["gb5"] = grad_gather(state["gb4"], yg_b, ygrec_b, full_b)
+
+    def s_ga6():
+        state["ga6"] = grad_core(state["ga5"], full_a)
+
+    def s_gb6():
+        state["gb6"] = grad_core(state["gb5"], full_b)
+
+    s_b()
+    s_coef()
 
     for copy in ogc:
         copy.wait_recv()
@@ -310,110 +419,22 @@
             xs[at : at + 2 * toks] = pair
             at += 2 * toks
 
-    def chunk_copy(k, src, dst, dev, j):
-        return pltpu.make_async_remote_copy(
-            src_ref=src.at[j], dst_ref=dst.at[j], send_sem=csend.at[k, j],
-            recv_sem=crecv.at[k, j], device_id=dev, device_id_type=pl.DeviceIdType.MESH,
-        )
-
-    def core_copy(j):
-        return chunk_copy(0, psend, prec, core, j)
-
-    def y_copy(j):
-        return chunk_copy(1, ysend, yrec, ynb, j)
-
-    def x_copy(j):
-        return chunk_copy(2, xsend, xrecv, xnb, j)
-
-    pair_rows = 2 * toks
-
-    def stage_matmul(j):
-        w_copy(j).wait()
-        part = nt(xs[...], wv[j])
-        for yr in (0, 1):
-            at = 2 * yr * pair_rows
-            keep[j, yr] = part[at : at + pair_rows]
-            psend[j, yr] = part[at + pair_rows : at + 2 * pair_rows].astype(bf16)
-        core_copy(j).start()
-
-    def stage_y(j):
-        core_copy(j).wait_recv()
-        ysend[j] = (keep[j, 1] + prec[j, 1].astype(f32)).astype(bf16)
-        y_copy(j).start()
-
-    def lora(at):
-        own = jnp.dot(coef_own, a_ref[0, :, at], preferred_element_type=f32)
-        oth = jnp.dot(coef_oth, aoth[:, at], preferred_element_type=f32)
-        return (adapter_scale * (own + oth)).astype(bf16).astype(f32)
-
-    def stage_x(j):
-        y_copy(j).wait_recv()
-        total = keep[j, 0] + prec[j, 0].astype(f32) + yrec[j].astype(f32)
-        xsend[j] = total[toks:].astype(bf16)
-        x_copy(j).start()
-        at = cols(a * half + j * ch, ch, ch)
-        own = total[:toks].astype(bf16).astype(f32)
-        out_ref[:, at] = (own + lora(at)).astype(bf16)
-
-    def stage_out(j):
-        x_copy(j).wait_recv()
-        at = cols((1 - a) * half + j * ch, ch, ch)
-        out_ref[:, at] = (xrecv[j].astype(f32) + lora(at)).astype(bf16)
-
-    def loop(first, last):
-        @pl.loop(first, last)
-        def _(j):
+    adapter_steps = [
+        [], [s_a], [s_low], [s_gb2], [], [s_ga3], [], [s_ga4, s_gb3], [s_gb4, s_ga5], [s_gb5],
+        [s_ga6, s_gb6],
+    ]
+    lag = 5
+    stage_matmul(0)
+    s_ga2()
+    for j in range(1, max(len(adapter_steps) + 1, chunks + lag)):
+        if j < chunks:
             stage_matmul(j)
+        if j <= chunks:
             stage_y(j - 1)
-
-    mid = min(chunks, 1 + chunks // 2)
-    stage_matmul(0)
-    loop(1, mid)
-    ga2 = grad_z(ga1, gkeep_a, grec_a, zs_a, zrec_a)
-    ax.wait_recv()
-    ap = go(remote(aoth.at[:, acols], aoth.at[:, acols], core))
-    loop(mid, chunks)
-    stage_y(chunks - 1)
-    ap.wait_recv()
-    low = masked_pair(hid_ref[...], a_ref[0], aoth[...])
-    low_t = jnp.transpose(low, (1, 0)).astype(bf16)
-    gb1 = grad_first(low_t, og_ref, gsend_b, gkeep_b, grec_b, hb)
-
-    state = {}
-
-    def s_gb2():
-        state["gb2"] = grad_z(gb1, gkeep_b, grec_b, zs_b, zrec_b)
-
-    def s_ga3():
-        state["ga3"] = grad_x(ga2, zs_a, zrec_a, sum_a, xg_a, xgrec_a)
-
-    def s_ga4():
-        state["ga4"] = grad_y(state["ga3"], sum_a, xgrec_a, yg_a, ygrec_a)
-
-    def s_gb3():
-        state["gb3"] = grad_x(state["gb2"], zs_b, zrec_b, sum_b, xg_b, xgrec_b)
-
-    def s_ga5():
-        state["ga5"] = grad_gather(state["ga4"], yg_a, ygrec_a, full_a)
-
-    def s_gb4():
-        state["gb4"] = grad_y(state["gb3"], sum_b, xgrec_b, yg_b, ygrec_b)
-
-    def s_gb5():
-        state["gb5"] = grad_gather(state["gb4"], yg_b, ygrec_b, full_b)
-
-    def s_ga6():
-        state["ga6"] = grad_core(state["ga5"], full_a)
-
-    def s_gb6():
-        state["gb6"] = grad_core(state["gb5"], full_b)
-
-    between = [[s_gb2], [s_ga3], [s_ga4, s_gb3], [s_gb4, s_ga5], [s_gb5], [s_ga6], [s_gb6]]
-    for j in range(max(chunks, len(between))):
-        if j < chunks:
-            stage_x(j)
-        if j < len(between):
-            for step in between[j]:
+        if lag <= j < chunks + lag:
+            stage_x(j - lag)
+        if j - 1 < len(adapter_steps):
+            for step in adapter_steps[j - 1]:
                 step()
     for j in range(chunks):
         stage_out(j)
@@ -425,6 +446,16 @@
         core_copy(j).wait_send()
         y_copy(j).wait_send()
         x_copy(j).wait_send()
+
+
+def finish_kernel(scale, base_ref, fa_ref, fb_ref, out_ref, ga_ref, gb_ref):
+    out_ref[...] = base_ref[...]
+    for full, ref in ((fa_ref, ga_ref), (fb_ref, gb_ref)):
+        halves, groups, _, width = full.shape
+        for h in range(halves):
+            for q in range(groups):
+                at = (h * groups + q) * width
+                ref[0, :, at : at + width] = scale * full[h, q].astype(jnp.float32)
 
 
 def fused_on_device(
@@ -459,18 +490,22 @@
             pltpu.VMEM((2, groups, rank, wq), bf16),
         ]
 
-    copies = 4 + 7 + 2 * (4 + 2 * (groups - 1))
+    copies = 4 + 7 + 2 * (3 + 2 * (groups - 1) + groups)
     vmem = pl.BlockSpec(memory_space=pltpu.VMEM)
-    return pl.pallas_call(
-        functools.partial(fused_kernel, scale, chunks),
+    parts = pl.pallas_call(
+        functools.partial(fused_kernel, chunks),
         out_shape=(
             jax.ShapeDtypeStruct((toks, hidden_width), bf16),
-            jax.ShapeDtypeStruct((1, rank, hidden_width), f32),
-            jax.ShapeDtypeStruct((1, rank, model_width), f32),
+            jax.ShapeDtypeStruct((2, groups, rank, hidden_width // (2 * groups)), bf16),
+            jax.ShapeDtypeStruct((2, groups, rank, model_width // (2 * groups)), bf16),
         ),
-        in_specs=[vmem, vmem, vmem, pl.BlockSpec(memory_space=pl.ANY), vmem, vmem],
+        in_specs=[vmem] + [pl.BlockSpec(memory_space=pltpu.HBM)] * 5,
         out_specs=(vmem, vmem, vmem),
         scratch_shapes=[
+            pltpu.VMEM((toks, model_width), bf16),
+            pltpu.VMEM((toks, hidden_width), bf16),
+            pltpu.VMEM((1, rank, hidden_width), bf16),
+            pltpu.VMEM((1, rank, model_width), bf16),
             pltpu.VMEM((chunks, ch, slab), bf16),
             pltpu.VMEM((2, 2, 2, toks, slab), bf16),
             pltpu.VMEM((8 * toks, slab), bf16),
@@ -485,17 +520,31 @@
             pltpu.VMEM((rank, model_width), bf16),
             *grad_scratch(hidden_width),
             *grad_scratch(model_width),
+            pltpu.SemaphoreType.DMA((4,)),
             pltpu.SemaphoreType.DMA((chunks,)),
             pltpu.SemaphoreType.DMA((copies,)),
             pltpu.SemaphoreType.DMA((copies,)),
             pltpu.SemaphoreType.DMA((3, chunks)),
             pltpu.SemaphoreType.DMA((3, chunks)),
         ],
-        compiler_params=pltpu.CompilerParams(collective_id=0, has_side_effects=True),
+        compiler_params=pltpu.CompilerParams(
+            collective_id=0, has_side_effects=True, vmem_limit_bytes=64500000
+        ),
     )(
-        adapter_index.reshape(toks, 1), output_gradient, hidden, frozen_down_weight,
+        adapter_index.reshape(1, toks), output_gradient, hidden, frozen_down_weight,
         adapter_input_maps, adapter_output_maps,
     )
+    return pl.pallas_call(
+        functools.partial(finish_kernel, scale),
+        out_shape=(
+            jax.ShapeDtypeStruct((toks, hidden_width), bf16),
+            jax.ShapeDtypeStruct((1, rank, hidden_width), f32),
+            jax.ShapeDtypeStruct((1, rank, model_width), f32),
+        ),
+        in_specs=[vmem] * 3,
+        out_specs=(vmem,) * 3,
+        compiler_params=pltpu.CompilerParams(vmem_limit_bytes=64500000),
+    )(*parts)
 
 
 def per_device(mesh):

time: 57.5 us -> 48.5 us (0.84)
  local copies, waits for them, and re-layouts: 7.15 us -> 0 us
  Pallas kernels: 49.5 us -> 47.7 us
    unnamed x3 -> x0, local copies, waits for them, and re-layouts: 5.82 us -> none
    pallas_call x1 -> x2, Pallas kernels: 49.5 us -> 47.7 us  [the longest x1 45.2 us: fused_on_device(): pl.pallas_call(functools.partial(fused_kernel, chunks), out_shape=(jax.Sh...]
    reshape x1 -> x0, local copies, waits for them, and re-layouts: 1.33 us -> none  [fused_on_device(): adapter_index.reshape(toks, 1)]
where the time goes in v2:
time: 48.5 us; the launch traced here: 48.4 us
  Pallas kernels  47.7 us (98%)
  between operations  0.64 us (1%)
    pallas_call x1, Pallas kernels, fused_on_device(): pl.pallas_call(functools.partial(fused_kernel, chunks), out_shape=(jax.Sh...  45.2 us
    pallas_call x1, Pallas kernels, fused_on_device(): pl.pallas_call(functools.partial(finish_kernel, scale), out_shape=(jax.Sh...  2.57 us

profile of v2, /device:TPU:0, one launch (start us, length us, event | category | flops | bytes accessed | tf_op | source)
XLA Modules:
  0.0 48.4 jit_solution(11726344851968242754)
XLA Ops:
  0.6 45.2 %shard_map.85 = (bf16[24,14336]{1,0:T(8,128)(2,1)}, bf16[2,4,16,1792]{3,2,1,0:T(8,128)(2,1)}, bf16[2,4,16,512]{3,2,1,0:T(8,128)(2,1)}) custom-call(s32[1,24]{1,0:T(1,128)} %bitcast.1, bf16[24,4096]{1,0:T(8,128)(2,1)} %og_hbm.1, bf16[24,14336]{1,0:T(8,128)(2,1)} %hid_hbm.1, bf16[7168,1024]{1,0:T(8,128)(2,1)} %w_ref.1, bf16[1,16,14336]{2,1,0:T(8,128)(2,1)} %a_hbm.1, ...), custom_call_target="tpu_custom_call" | custom-call | tf_op jit(solution)/shard_map/pallas_call | solution.py:495
  45.8 2.6 %shard_map.86 = (bf16[24,14336]{1,0:T(8,128)(2,1)}, f32[1,16,14336]{2,1,0:T(8,128)}, f32[1,16,4096]{2,1,0:T(8,128)}) custom-call(bf16[24,14336]{1,0:T(8,128)(2,1)} %get-tuple-element.6.base_ref, bf16[2,4,16,1792]{3,2,1,0:T(8,128)(2,1)} %get-tuple-element.7.fa_ref, bf16[2,4,16,512]{3,2,1,0:T(8,128)(2,1)} %get-tuple-element.8.fb_ref), custom_call_target="tpu_custom_call" | custom-call | tf_op jit(solution)/shard_map/pallas_call | solution.py:537
